TPU v7x, 32 devices: a whole 2x2x4 slice. The times are simulated.
32 devices in a mesh: expert: 8 (over z, y), dp: 4 (over x, core).
Axes of the slice: x: 2, y: 2, z: 4, core: 2. Of those that a mesh axis runs over, the one named last changes fastest.
Arguments:
- grad_parts: bfloat16 [4, 8, 3584, 1024], P('dp', 'expert'), may hold values from -6 to 6
- owner_slot: int32 [8], replicated, may hold values from 0 to 7, each once
- slot_expert: int32 [8, 2], replicated, may hold values from 0 to 7, all different within a row
- master: float32 [8, 3584, 1024], P(None, 'expert', 'dp'), may hold values from -1.5 to 1.5
- moment_one: float32 [8, 3584, 1024], P(None, 'expert', 'dp'), may hold values from -2 to 2
- moment_two: float32 [8, 3584, 1024], P(None, 'expert', 'dp'), may hold values from 0.01 to 1
- ema_weights: float32 [8, 3584, 1024], P(None, 'expert', 'dp'), may hold values from -1.5 to 1.5
Outputs:
- master_out: float32 [8, 3584, 1024], P(None, 'expert', 'dp')
- moment_one_out: float32 [8, 3584, 1024], P(None, 'expert', 'dp')
- moment_two_out: float32 [8, 3584, 1024], P(None, 'expert', 'dp')
- ema_out: float32 [8, 3584, 1024], P(None, 'expert', 'dp')
- replicas: bfloat16 [16, 3584, 1024], P('expert', None, 'dp')
Inputs may be any that keep to these rules, and one draw needn't show every extreme that they name: `owner_slot`: a permutation of the 8 experts; position k belongs to expert-axis index k. `slot_expert`: each row names 2 different experts, and every expert is named by some row.
All inputs are finite; a program needn't handle non-finite values.
Results may differ from a plain program's by a relative error of at most 0.009.
Values may be sent and summed in bfloat16 or wider, within the bound.
A program may use at most 128 MiB of HBM per device.

v0:
```python
import jax
import jax.numpy as jnp
from jax import lax
from jax.sharding import PartitionSpec as P

STEP = 10
beta_one = 0.9
beta_two = 0.999
adam_eps = 1e-08
learn_rate = 0.05
decay_rate = 0.1
ema_decay = 0.99


def per_device(grad_parts, owner_slot, slot_expert, master, moment_one, moment_two, ema_weights):
    summed = lax.psum_scatter(
        grad_parts[0].astype(jnp.float32).astype(jnp.bfloat16),
        "dp",
        scatter_dimension=2,
        tiled=True,
    ).astype(jnp.float32)
    owner_rows = lax.all_to_all(
        summed.astype(jnp.bfloat16), "expert", split_axis=1, concat_axis=0, tiled=True
    ).astype(summed.dtype)
    gradient = jnp.take(owner_rows, owner_slot, axis=0)
    correct_one = 1.0 - beta_one**STEP
    correct_two = 1.0 - beta_two**STEP
    moment_one_out = beta_one * moment_one + (1.0 - beta_one) * gradient
    moment_two_out = beta_two * moment_two + (1.0 - beta_two) * gradient * gradient
    update = moment_one_out / correct_one / (jnp.sqrt(moment_two_out / correct_two) + adam_eps)
    master_out = master - learn_rate * (update + decay_rate * master)
    ema_out = ema_decay * ema_weights + (1.0 - ema_decay) * master_out
    updated_bf16 = master_out.astype(jnp.bfloat16)
    outgoing = jnp.take(updated_bf16, slot_expert.reshape(-1), axis=0)
    replicas = lax.all_to_all(outgoing, "expert", split_axis=0, concat_axis=1, tiled=True)
    return (master_out, moment_one_out, moment_two_out, ema_out, replicas)


def solution(mesh):
    placed = (
        P("dp", "expert", None, None),
        P(),
        P(),
        P(None, "expert", "dp"),
        P(None, "expert", "dp"),
        P(None, "expert", "dp"),
        P(None, "expert", "dp"),
    )
    return jax.shard_map(
        per_device,
        mesh=mesh,
        in_specs=placed,
        out_specs=(
            P(None, "expert", "dp"),
            P(None, "expert", "dp"),
            P(None, "expert", "dp"),
            P(None, "expert", "dp"),
            P("expert", None, "dp"),
        ),
        check_vma=False,
    )
```

profile of v0, /device:TPU:0, one launch (start us, length us, event | category | flops | bytes accessed | tf_op | source)
XLA Modules:
  0.0 281.6 jit_solution(11911839623130922514)
XLA Ops:
  7.2 0.0 reduce-scatter.2.cloned.1.call-start
  7.2 0.7 reduce-scatter.2.cloned.1.call-update
  7.9 69.9 %reduce-scatter.2.cloned.1.call-done = bf16[1,3584,256]{2,1,0:T(8,128)(2,1)} async-done(((bf16[1,3584,1024]{2,1,0:T(8,128)(2,1)}), bf16[1,3584,256]{2,1,0:T(8,128)(2,1)}) %reduce-scatter.2.cloned.1.call-update) | async-done | bytes 1835024 | tf_op jit(solution)/shard_map/reduce_scatter | solution.py:16
  77.8 6.8 %copy.27 = bf16[1,3584,256]{2,0,1:T(2,128)(2,1)} copy(bf16[1,3584,256]{2,1,0:T(8,128)(2,1)} %reduce-scatter.2.cloned.1.call-done) | data formatting | bytes 3670016 | tf_op jit(solution)/shard_map/reduce_scatter | solution.py:16
  84.6 0.5 broadcast.61
  85.1 19.1 %reduce = bf16[3584,256]{1,0:T(8,128)(2,1)S(1)} reduce(bf16[3584,1,256]{2,1,0:T(2,128)(2,1)} %bitcast.14, bf16[]{:T(256)} %broadcast.61), dimensions={1}, to_apply=%bitcast.11.reduce_sub_computation | reduce | bytes 3670018
  104.2 0.0 copy-start
  104.2 0.0 copy-start.1
  104.2 3.1 %reshape.79 = bf16[8,2,57344]{2,1,0:T(2,128)(2,1)} reshape(bf16[3584,256]{1,0:T(8,128)(2,1)S(1)} %reduce) | data formatting | bytes 3670016
  107.3 5.5 %all-to-all-start = ((bf16[8,2,57344]{2,1,0:T(2,128)(2,1)}), bf16[8,2,57344]{2,1,0:T(2,128)(2,1)S(1)}, u32[]{:S(2)}, u32[]{:S(2)}) async-start(bf16[8,2,57344]{2,1,0:T(2,128)(2,1)} %reshape.79), calls=%async_computation.1 | async-start | bytes 3670016 | tf_op jit(solution)/shard_map/all_to_all | solution.py:22
  112.9 0.1 copy.22
  112.9 0.1 reshape.60
  113.0 0.1 reshape.59
  113.2 42.2 %all-to-all-done = bf16[8,2,57344]{2,1,0:T(2,128)(2,1)S(1)} async-done(((bf16[8,2,57344]{2,1,0:T(2,128)(2,1)}), bf16[8,2,57344]{2,1,0:T(2,128)(2,1)S(1)}, u32[]{:S(2)}, u32[]{:S(2)}) %all-to-all-start) | async-done | bytes 1835040 | tf_op jit(solution)/shard_map/all_to_all | solution.py:22
  155.3 4.1 %reshape.80 = bf16[3584,1,256]{2,1,0:T(2,128)(2,1)} reshape(bf16[8,2,57344]{2,1,0:T(2,128)(2,1)S(1)} %all-to-all-done) | data formatting | bytes 3670016
  159.4 4.1 %copy.25 = f32[1,3584,256]{2,1,0:T(8,128)} copy(bf16[1,3584,256]{2,0,1:T(2,128)(2,1)} %bitcast.13) | data formatting | bytes 5505024
  163.5 4.7 %gather_fusion = f32[8,448,256]{2,1,0:T(8,128)} fusion(f32[8,448,256]{2,1,0:T(8,128)} %bitcast.12, s32[1024]{0:T(1024)S(1)} %pad_clamp_fusion.1), kind=kCustom, calls=%fused_computation | custom fusion | bytes 7340064 | tf_op jit(solution)/shard_map/jit(_take)/gather | solution.py:25
  168.2 9.6 %fusion.2 = (bf16[8,448,256]{2,1,0:T(8,128)(2,1)S(1)}, f32[8,448,256]{2,1,0:T(8,128)}, f32[8,448,256]{2,1,0:T(8,128)}, f32[8,448,256]{2,1,0:T(8,128)}) fusion(f32[8,448,256]{2,1,0:T(8,128)} %param.10, f32[8,448,256]{2,1,0:T(8,128)} %gather_fusion, pred[8]{0:T(512)(128)(4,1)S(1)} %compare_and_fusion.1, f32[8,448,256]{2,1,0:T(8,128)} %param.11, ...), kind=kLoop, calls=%fused_computation.16 | loop fusion | flops 15597568 | bytes 27525128 | tf_op jit(solution)/shard_map/convert_element_type | solution.py:33
  177.7 2.6 gather_fusion.1
  180.4 4.3 %broadcast_select_fusion = bf16[16,448,256]{2,1,0:T(8,128)(2,1)} fusion(bf16[16,448,256]{2,1,0:T(8,128)(2,1)} %gather_fusion.1, pred[16]{0:T(512)(128)(4,1)S(1)} %compare_and_fusion), kind=kLoop, calls=%fused_computation.7 | loop fusion | flops 1835008 | bytes 7340048 | tf_op jit(solution)/shard_map/jit(_take)/select_n | solution.py:34
  184.6 4.5 %all-to-all-start.1 = ((bf16[16,448,256]{2,1,0:T(8,128)(2,1)}), bf16[16,448,256]{2,1,0:T(8,128)(2,1)}, u32[]{:S(2)}, u32[]{:S(2)}) async-start(bf16[16,448,256]{2,1,0:T(8,128)(2,1)} %broadcast_select_fusion), calls=%async_computation.2 | async-start | bytes 7340032 | tf_op jit(solution)/shard_map/all_to_all | solution.py:35
  189.1 5.6 %multiply_add_fusion = f32[8,448,256]{2,1,0:T(8,128)} fusion(f32[8,448,256]{2,1,0:T(8,128)} %get-tuple-element.6, f32[8,448,256]{2,1,0:T(8,128)} %param.13), kind=kLoop, calls=%fused_computation.4 | loop fusion | flops 2752512 | bytes 11010048 | tf_op jit(solution)/shard_map/add | solution.py:32
  194.7 75.8 %all-to-all-done.1 = bf16[16,448,256]{2,1,0:T(8,128)(2,1)} async-done(((bf16[16,448,256]{2,1,0:T(8,128)(2,1)}), bf16[16,448,256]{2,1,0:T(8,128)(2,1)}, u32[]{:S(2)}, u32[]{:S(2)}) %all-to-all-start.1) | async-done | bytes 3670048 | tf_op jit(solution)/shard_map/all_to_all | solution.py:35
  270.5 4.2 %copy.24 = bf16[2,8,448,256]{3,2,1,0:T(8,128)(2,1)} copy(bf16[2,8,448,256]{3,2,0,1:T(8,128)(2,1)} %bitcast.3) | data formatting | bytes 7340032 | tf_op jit(solution)/shard_map/all_to_all | solution.py:35
  (8 shorter events, 0.0 us)
Async XLA Ops:
  7.2 70.7 %reduce-scatter.2.cloned.1.call-start = ((), (), s32[]{:S(2)}) async-start(), calls=%async_computation.3 | async-start | bytes 9175040 | tf_op jit(solution)/shard_map/reduce_scatter | solution.py:16
  104.2 8.6 %copy-start = (s32[8,2]{0,1:T(2,128)S(1)}, s32[8,2]{0,1:T(2,128)}, u32[]{:S(2)}) copy-start(s32[8,2]{0,1:T(2,128)} %param.9) | copy-start | bytes 196
  104.2 8.9 %copy-start.1 = (s32[8]{0:T(128)S(1)}, s32[8]{0:T(128)}, u32[]{:S(2)}) copy-start(s32[8]{0:T(128)} %param.8) | copy-start | bytes 100
  107.3 48.0 %all-to-all-start = ((bf16[8,2,57344]{2,1,0:T(2,128)(2,1)}), bf16[8,2,57344]{2,1,0:T(2,128)(2,1)S(1)}, u32[]{:S(2)}, u32[]{:S(2)}) async-start(bf16[8,2,57344]{2,1,0:T(2,128)(2,1)} %reshape.79), calls=%async_computation.1 | async-start | bytes 3670016 | tf_op jit(solution)/shard_map/all_to_all | solution.py:22
  184.6 85.9 %all-to-all-start.1 = ((bf16[16,448,256]{2,1,0:T(8,128)(2,1)}), bf16[16,448,256]{2,1,0:T(8,128)(2,1)}, u32[]{:S(2)}, u32[]{:S(2)}) async-start(bf16[16,448,256]{2,1,0:T(8,128)(2,1)} %broadcast_select_fusion), calls=%async_computation.2 | async-start | bytes 7340032 | tf_op jit(solution)/shard_map/all_to_all | solution.py:35
Sparse Core Ops, SparseCore 0:
  10.5 67.2 reduce-scatter.1
where the time goes:
time: 282 us
  waiting for transfers between devices  189 us (67%)
  other arithmetic  38.6 us (14%)
  local copies, waits for them, and re-layouts  30.3 us (11%)
  between operations  14.1 us (5%)
  starting transfers between devices  10 us (4%)
    all_to_all x1, waiting for transfers between devices, per_device(): lax.all_to_all(outgoing, 'expert', split_axis=0, concat_axis=1, tiled=True)  75.8 us
    reduce_scatter x1, waiting for transfers between devices, per_device(): lax.psum_scatter(grad_parts[0].astype(jnp.float32).astype(jnp.bfloat16),...  69.9 us
    all_to_all x1, waiting for transfers between devices, per_device(): lax.all_to_all(summed.astype(jnp.bfloat16), 'expert', split_axis=1, conca...  42.2 us
    unnamed x1, other arithmetic  19.1 us
    unnamed x9, local copies, waits for them, and re-layouts  11.9 us
    convert_element_type x1, other arithmetic, per_device(): updated_bf16 = master_out.astype(jnp.bfloat16)  9.56 us
    reduce_scatter x1, local copies, waits for them, and re-layouts, per_device(): lax.psum_scatter(grad_parts[0].astype(jnp.float32).astype(jnp.bfloat16),...  6.77 us
  transfers between devices with their start and end apart: 3, of which 3 were waited for; matrix products, arithmetic and copies ran while one was open for 2% of the time, Pallas kernels for 0%

commit v1 on v0

--- a/solution.py
+++ b/solution.py
@@ -12,6 +12,18 @@
 ema_decay = 0.99
 
 
+def rotated_exchange(x, axis, split, join):
+    ways, here = (lax.axis_size(axis), lax.axis_index(axis))
+    width = x.shape[split] // ways
+    turned = jnp.roll(x, -here * width, axis=split)
+    got = [lax.slice_in_dim(turned, 0, width, axis=split)]
+    for far in range(1, ways):
+        sent = lax.slice_in_dim(turned, far * width, (far + 1) * width, axis=split)
+        got.append(lax.ppermute(sent, axis, [(d, (d + far) % ways) for d in range(ways)]))
+    line = jnp.concatenate(got[::-1], axis=join)
+    return jnp.roll(line, (here + 1) * got[0].shape[join], axis=join)
+
+
 def per_device(grad_parts, owner_slot, slot_expert, master, moment_one, moment_two, ema_weights):
     summed = lax.psum_scatter(
         grad_parts[0].astype(jnp.float32).astype(jnp.bfloat16),
@@ -19,9 +31,7 @@
         scatter_dimension=2,
         tiled=True,
     ).astype(jnp.float32)
-    owner_rows = lax.all_to_all(
-        summed.astype(jnp.bfloat16), "expert", split_axis=1, concat_axis=0, tiled=True
-    ).astype(summed.dtype)
+    owner_rows = rotated_exchange(summed.astype(jnp.bfloat16), "expert", 1, 0).astype(summed.dtype)
     gradient = jnp.take(owner_rows, owner_slot, axis=0)
     correct_one = 1.0 - beta_one**STEP
     correct_two = 1.0 - beta_two**STEP

time: 282 us -> 247 us (0.88)
  local copies, waits for them, and re-layouts: 30.3 us -> 12.1 us
  other arithmetic: 38.6 us -> 24.7 us
  waiting for transfers between devices: 189 us -> 179 us
  starting transfers between devices: 10 us -> 16.8 us
    all_to_all x1 -> x0, waiting for transfers between devices: 42.2 us -> none  [per_device(): lax.all_to_all(summed.astype(jnp.bfloat16), 'expert', split_axis=1, conca...]
    ppermute x0 -> x7, waiting for transfers between devices: none -> 32.2 us  [rotated_exchange(): lax.ppermute(sent, axis, [(d, (d + far) % ways) for d in range(ways)])]
    unnamed x1 -> x0, other arithmetic: 19.1 us -> none
    unnamed x9 -> x20, local copies, waits for them, and re-layouts: 11.9 us -> 0.34 us
    ppermute x0 -> x7, starting transfers between devices: none -> 11.2 us  [rotated_exchange(): lax.ppermute(sent, axis, [(d, (d + far) % ways) for d in range(ways)])]
    reduce_scatter x1 -> x0, local copies, waits for them, and re-layouts: 6.77 us -> none  [per_device(): lax.psum_scatter(grad_parts[0].astype(jnp.float32).astype(jnp.bfloat16),...]
    all_to_all x1 -> x0, starting transfers between devices: 5.52 us -> none  [per_device(): lax.all_to_all(summed.astype(jnp.bfloat16), 'expert', split_axis=1, conca...]
    concatenate x0 -> x1, other arithmetic: none -> 3.09 us  [rotated_exchange(): turned = jnp.roll(x, -here * width, axis=split)]
  transfers between devices with their start and end apart: 3 -> 9, of which waited for: 3 -> 6; matrix products, arithmetic and copies ran while one was open for 2% -> 2% of each run, Pallas kernels for 0% -> 0%
where the time goes in v1:
time: 247 us
  waiting for transfers between devices  179 us (72%)
  other arithmetic  24.7 us (10%)
  starting transfers between devices  16.8 us (7%)
  between operations  14.3 us (6%)
  local copies, waits for them, and re-layouts  12.1 us (5%)
    all_to_all x1, waiting for transfers between devices, per_device(): lax.all_to_all(outgoing, 'expert', split_axis=0, concat_axis=1, tiled=True)  76.7 us
    reduce_scatter x1, waiting for transfers between devices, per_device(): lax.psum_scatter(grad_parts[0].astype(jnp.float32).astype(jnp.bfloat16),...  69.6 us
    ppermute x7, waiting for transfers between devices, rotated_exchange(): lax.ppermute(sent, axis, [(d, (d + far) % ways) for d in range(ways)])  32.2 us
    ppermute x7, starting transfers between devices, rotated_exchange(): lax.ppermute(sent, axis, [(d, (d + far) % ways) for d in range(ways)])  11.2 us
    convert_element_type x1, other arithmetic, per_device(): updated_bf16 = master_out.astype(jnp.bfloat16)  9.56 us
    all_to_all x1, starting transfers between devices, per_device(): lax.all_to_all(outgoing, 'expert', split_axis=0, concat_axis=1, tiled=True)  5.61 us
    add x1, other arithmetic, per_device(): ema_out = ema_decay * ema_weights + (1.0 - ema_decay) * master_out  5.58 us
  transfers between devices with their start and end apart: 9, of which 6 were waited for; matrix products, arithmetic and copies ran while one was open for 2% of the time, Pallas kernels for 0%

profile of v1, /device:TPU:0, one launch (start us, length us, event | category | flops | bytes accessed | tf_op | source)
XLA Modules:
  0.0 247.0 jit_solution(2521211663224226463)
XLA Ops:
  7.2 0.7 reduce-scatter.2.cloned.1.call-update
  8.2 69.6 %reduce-scatter.2.cloned.1.call-done = bf16[1,3584,256]{2,1,0:T(8,128)(2,1)} async-done(((bf16[1,3584,1024]{2,1,0:T(8,128)(2,1)}), bf16[1,3584,256]{2,1,0:T(8,128)(2,1)}) %reduce-scatter.2.cloned.1.call-update) | async-done | bytes 1835024 | tf_op jit(solution)/shard_map/reduce_scatter | solution.py:28
  77.8 3.1 %fusion.1 = bf16[1,3584,256]{2,1,0:T(8,128)(2,1)S(1)} fusion(s32[]{:T(128)S(6)} %select_n.54, bf16[1,3584,256]{2,1,0:T(8,128)(2,1)} %reduce-scatter.2.cloned.1.call-done), kind=kLoop, calls=%fused_computation.10 | loop fusion | flops 3670016 | bytes 3670020 | tf_op jit(solution)/shard_map/jit(_roll_dynamic)/concatenate | solution.py:18
  80.9 0.1 fusion.5
  81.1 4.4 %collective-permute-start = (bf16[1,448,256]{2,1,0:T(8,128)(2,1)S(1)}, bf16[1,448,256]{2,1,0:T(8,128)(2,1)S(1)}, u32[]{:S(2)}, u32[]{:S(2)}) collective-permute-start(bf16[1,448,256]{2,1,0:T(8,128)(2,1)S(1)} %get-tuple-element.15), channel_id=1, source_target_pairs={{0,28},{4,0},{8,4},{12,8},{16,12},{20,16},{24,20},{28,24},{1,29},{... | collective-permute-start | bytes 688136 | tf_op jit(solution)/shard_map/ppermute | solution.py:22
  85.4 0.5 collective-permute-start.1
  85.9 0.6 collective-permute-start.6
  86.5 1.0 collective-permute-start.5
  87.5 0.9 collective-permute-start.4
  88.4 3.0 %collective-permute-done = bf16[1,448,256]{2,1,0:T(8,128)(2,1)S(1)} collective-permute-done((bf16[1,448,256]{2,1,0:T(8,128)(2,1)S(1)}, bf16[1,448,256]{2,1,0:T(8,128)(2,1)S(1)}, u32[]{:S(2)}, u32[]{:S(2)}) %collective-permute-start) | collective-permute-done | bytes 229408 | tf_op jit(solution)/shard_map/ppermute | solution.py:22
  91.4 2.4 collective-permute-start.2
  93.8 2.5 %collective-permute-done.1 = bf16[1,448,256]{2,1,0:T(8,128)(2,1)S(1)} collective-permute-done((bf16[1,448,256]{2,1,0:T(8,128)(2,1)S(1)}, bf16[1,448,256]{2,1,0:T(8,128)(2,1)S(1)}, u32[]{:S(2)}, u32[]{:S(2)}) %collective-permute-start.1) | collective-permute-done | bytes 229408 | tf_op jit(solution)/shard_map/ppermute | solution.py:22
  96.4 1.5 collective-permute-start.3
  97.8 13.3 %collective-permute-done.2 = bf16[1,448,256]{2,1,0:T(8,128)(2,1)S(1)} collective-permute-done((bf16[1,448,256]{2,1,0:T(8,128)(2,1)S(1)}, bf16[1,448,256]{2,1,0:T(8,128)(2,1)S(1)}, u32[]{:S(2)}, u32[]{:S(2)}) %collective-permute-start.2) | collective-permute-done | bytes 229408 | tf_op jit(solution)/shard_map/ppermute | solution.py:22
  111.2 13.3 %collective-permute-done.3 = bf16[1,448,256]{2,1,0:T(8,128)(2,1)S(1)} collective-permute-done((bf16[1,448,256]{2,1,0:T(8,128)(2,1)S(1)}, bf16[1,448,256]{2,1,0:T(8,128)(2,1)S(1)}, u32[]{:S(2)}, u32[]{:S(2)}) %collective-permute-start.3) | collective-permute-done | bytes 229408 | tf_op jit(solution)/shard_map/ppermute | solution.py:22
  124.8 2.2 dynamic-slice_convert_fusion
  127.0 4.7 %gather_fusion = f32[8,448,256]{2,1,0:T(8,128)} fusion(f32[8,448,256]{2,1,0:T(8,128)} %dynamic-slice_convert_fusion, s32[1024]{0:T(1024)S(1)} %get-tuple-element.17), kind=kCustom, calls=%fused_computation | custom fusion | bytes 7340064 | tf_op jit(solution)/shard_map/jit(_take)/gather | solution.py:35
  131.7 9.6 %fusion.3 = (bf16[8,448,256]{2,1,0:T(8,128)(2,1)S(1)}, f32[8,448,256]{2,1,0:T(8,128)}, f32[8,448,256]{2,1,0:T(8,128)}, f32[8,448,256]{2,1,0:T(8,128)}) fusion(f32[8,448,256]{2,1,0:T(8,128)} %param.10, f32[8,448,256]{2,1,0:T(8,128)} %gather_fusion, pred[8]{0:T(512)(128)(4,1)S(1)} %compare_and_fusion.1, f32[8,448,256]{2,1,0:T(8,128)} %param.11, ...), kind=kLoop, calls=%fused_computation.36 | loop fusion | flops 15597568 | bytes 27525128 | tf_op jit(solution)/shard_map/convert_element_type | solution.py:43
  141.2 2.6 %gather_fusion.1 = bf16[16,448,256]{2,1,0:T(8,128)(2,1)} fusion(bf16[8,448,256]{2,1,0:T(8,128)(2,1)S(1)} %get-tuple-element.5, s32[1024]{0:T(1024)S(1)} %get-tuple-element.16), kind=kCustom, calls=%fused_computation.1 | custom fusion | bytes 7340096 | tf_op jit(solution)/shard_map/jit(_take)/gather | solution.py:44
  143.8 4.3 %broadcast_select_fusion = bf16[16,448,256]{2,1,0:T(8,128)(2,1)} fusion(bf16[16,448,256]{2,1,0:T(8,128)(2,1)} %gather_fusion.1, pred[16]{0:T(512)(128)(4,1)S(1)} %compare_and_fusion), kind=kLoop, calls=%fused_computation.9 | loop fusion | flops 1835008 | bytes 7340048 | tf_op jit(solution)/shard_map/jit(_take)/select_n | solution.py:44
  148.1 5.6 %all-to-all-start = ((bf16[16,448,256]{2,1,0:T(8,128)(2,1)}), bf16[16,448,256]{2,1,0:T(8,128)(2,1)}, u32[]{:S(2)}, u32[]{:S(2)}) async-start(bf16[16,448,256]{2,1,0:T(8,128)(2,1)} %broadcast_select_fusion), calls=%async_computation.1 | async-start | bytes 7340032 | tf_op jit(solution)/shard_map/all_to_all | solution.py:45
  153.7 5.6 %multiply_add_fusion = f32[8,448,256]{2,1,0:T(8,128)} fusion(f32[8,448,256]{2,1,0:T(8,128)} %get-tuple-element.6, f32[8,448,256]{2,1,0:T(8,128)} %param.13), kind=kLoop, calls=%fused_computation.6 | loop fusion | flops 2752512 | bytes 11010048 | tf_op jit(solution)/shard_map/add | solution.py:42
  159.3 76.7 %all-to-all-done = bf16[16,448,256]{2,1,0:T(8,128)(2,1)} async-done(((bf16[16,448,256]{2,1,0:T(8,128)(2,1)}), bf16[16,448,256]{2,1,0:T(8,128)(2,1)}, u32[]{:S(2)}, u32[]{:S(2)}) %all-to-all-start) | async-done | bytes 3670048 | tf_op jit(solution)/shard_map/all_to_all | solution.py:45
  236.0 4.2 %copy.17 = bf16[2,8,448,256]{3,2,1,0:T(8,128)(2,1)} copy(bf16[2,8,448,256]{3,2,0,1:T(8,128)(2,1)} %bitcast.3) | data formatting | bytes 7340032 | tf_op jit(solution)/shard_map/all_to_all | solution.py:45
  (32 shorter events, 0.6 us)
Async XLA Ops:
  7.2 70.7 %reduce-scatter.2.cloned.1.call-start = ((), (), s32[]{:S(2)}) async-start(), calls=%async_computation.2 | async-start | bytes 9175040 | tf_op jit(solution)/shard_map/reduce_scatter | solution.py:28
  7.2 0.7 copy-start
  7.2 1.0 copy-start.1
  81.1 10.4 %collective-permute-start = (bf16[1,448,256]{2,1,0:T(8,128)(2,1)S(1)}, bf16[1,448,256]{2,1,0:T(8,128)(2,1)S(1)}, u32[]{:S(2)}, u32[]{:S(2)}) collective-permute-start(bf16[1,448,256]{2,1,0:T(8,128)(2,1)S(1)} %get-tuple-element.15), channel_id=1, source_target_pairs={{0,28},{4,0},{8,4},{12,8},{16,12},{20,16},{24,20},{28,24},{1,29},{... | collective-permute-start | bytes 688136 | tf_op jit(solution)/shard_map/ppermute | solution.py:22
  85.4 10.9 %collective-permute-start.1 = (bf16[1,448,256]{2,1,0:T(8,128)(2,1)S(1)}, bf16[1,448,256]{2,1,0:T(8,128)(2,1)S(1)}, u32[]{:S(2)}, u32[]{:S(2)}) collective-permute-start(bf16[1,448,256]{2,1,0:T(8,128)(2,1)S(1)} %get-tuple-element.14), channel_id=1, source_target_pairs={{0,24},{4,28},{8,0},{12,4},{16,8},{20,12},{24,16},{28,20},{1,25},{... | collective-permute-start | bytes 688136 | tf_op jit(solution)/shard_map/ppermute | solution.py:22
  85.9 38.7 %collective-permute-start.6 = (bf16[1,448,256]{2,1,0:T(8,128)(2,1)S(1)}, bf16[1,448,256]{2,1,0:T(8,128)(2,1)S(1)}, u32[]{:S(2)}, u32[]{:S(2)}) collective-permute-start(bf16[1,448,256]{2,1,0:T(8,128)(2,1)S(1)} %get-tuple-element.9), channel_id=1, source_target_pairs={{0,4},{4,8},{8,12},{12,16},{16,20},{20,24},{24,28},{28,0},{1,5},{5... | collective-permute-start | bytes 688136 | tf_op jit(solution)/shard_map/ppermute | solution.py:22
  86.5 38.1 %collective-permute-start.5 = (bf16[1,448,256]{2,1,0:T(8,128)(2,1)S(1)}, bf16[1,448,256]{2,1,0:T(8,128)(2,1)S(1)}, u32[]{:S(2)}, u32[]{:S(2)}) collective-permute-start(bf16[1,448,256]{2,1,0:T(8,128)(2,1)S(1)} %get-tuple-element.10), channel_id=1, source_target_pairs={{0,8},{4,12},{8,16},{12,20},{16,24},{20,28},{24,0},{28,4},{1,9},{5... | collective-permute-start | bytes 688136 | tf_op jit(solution)/shard_map/ppermute | solution.py:22
  87.5 37.0 %collective-permute-start.4 = (bf16[1,448,256]{2,1,0:T(8,128)(2,1)S(1)}, bf16[1,448,256]{2,1,0:T(8,128)(2,1)S(1)}, u32[]{:S(2)}, u32[]{:S(2)}) collective-permute-start(bf16[1,448,256]{2,1,0:T(8,128)(2,1)S(1)} %get-tuple-element.11), channel_id=1, source_target_pairs={{0,12},{4,16},{8,20},{12,24},{16,28},{20,0},{24,4},{28,8},{1,13},{... | collective-permute-start | bytes 688136 | tf_op jit(solution)/shard_map/ppermute | solution.py:22
  91.4 19.7 %collective-permute-start.2 = (bf16[1,448,256]{2,1,0:T(8,128)(2,1)S(1)}, bf16[1,448,256]{2,1,0:T(8,128)(2,1)S(1)}, u32[]{:S(2)}, u32[]{:S(2)}) collective-permute-start(bf16[1,448,256]{2,1,0:T(8,128)(2,1)S(1)} %get-tuple-element.13), channel_id=1, source_target_pairs={{0,20},{4,24},{8,28},{12,0},{16,4},{20,8},{24,12},{28,16},{1,21},{... | collective-permute-start | bytes 688136 | tf_op jit(solution)/shard_map/ppermute | solution.py:22
  96.4 28.1 %collective-permute-start.3 = (bf16[1,448,256]{2,1,0:T(8,128)(2,1)S(1)}, bf16[1,448,256]{2,1,0:T(8,128)(2,1)S(1)}, u32[]{:S(2)}, u32[]{:S(2)}) collective-permute-start(bf16[1,448,256]{2,1,0:T(8,128)(2,1)S(1)} %get-tuple-element.12), channel_id=1, source_target_pairs={{0,16},{4,20},{8,24},{12,28},{16,0},{20,4},{24,8},{28,12},{1,17},{... | collective-permute-start | bytes 688136 | tf_op jit(solution)/shard_map/ppermute | solution.py:22
  148.1 87.8 %all-to-all-start = ((bf16[16,448,256]{2,1,0:T(8,128)(2,1)}), bf16[16,448,256]{2,1,0:T(8,128)(2,1)}, u32[]{:S(2)}, u32[]{:S(2)}) async-start(bf16[16,448,256]{2,1,0:T(8,128)(2,1)} %broadcast_select_fusion), calls=%async_computation.1 | async-start | bytes 7340032 | tf_op jit(solution)/shard_map/all_to_all | solution.py:45
Sparse Core Ops, SparseCore 0:
  10.5 67.2 reduce-scatter.1
